TPU v7x, 512 devices: a whole 4x4x16 slice. The times are simulated.
512 devices in a mesh: space: 64 (over z, x_lo, core), tm: 8 (over x_hi, y).
Axes of the slice: x: 4 (x_hi: 2, x_lo: 2; x = x_hi * 2 + x_lo), y: 4, z: 16, core: 2. Of those that a mesh axis runs over, the one named last changes fastest.
Arguments:
- snapshots: bfloat16 [131072, 8192], P('space', 'tm'), may hold values from -30 to 30
- omega: int32 [32, 8192], P(None, 'tm'), may hold values from -1 to 1, as said below
Outputs:
- sketch: bfloat16 [32, 131072], P(None, 'space')
- coefficients: float32 [32, 8192], P(None, 'tm')
Inputs may be any that keep to these rules, and one draw needn't show every extreme that they name: `omega`: every entry is -1 or 1.
All inputs are finite; a program needn't handle non-finite values.
Results may differ from a plain program's by a relative error of at most 0.0028.
Values may be sent and summed in bfloat16 or wider, within the bound.
A program may use at most 64 MiB of HBM per device.

v0:
```python
import jax
import jax.numpy as jnp
from jax import lax
from jax.sharding import PartitionSpec as P

SNAP = 8192


def per_device(snapshots, omega):
    signs = omega.astype(jnp.bfloat16)
    partial_sums = lax.dot_general(
        signs, snapshots, (((1,), (1,)), ((), ())), preferred_element_type=jnp.float32
    )
    factor = SNAP ** (-0.5)
    summed = lax.psum(partial_sums, "tm")
    sketch = (summed * factor).astype(jnp.bfloat16)
    gram_part = lax.dot_general(
        sketch, sketch, (((1,), (1,)), ((), ())), preferred_element_type=jnp.float32
    )
    proj_part = jnp.dot(sketch, snapshots, preferred_element_type=jnp.float32)
    gram = lax.psum(gram_part, "space")
    projection = lax.psum(proj_part, "space")
    lower = jnp.linalg.cholesky(gram)
    coefficients = jax.scipy.linalg.solve_triangular(lower, projection, lower=True)
    return (sketch, coefficients)


def solution(mesh):
    placed = (P("space", "tm"), P(None, "tm"))
    return jax.shard_map(
        per_device,
        mesh=mesh,
        in_specs=placed,
        out_specs=(P(None, "space"), P(None, "tm")),
        check_vma=False,
    )
```

profile of v0, /device:TPU:1, one launch (start us, length us, event | category | flops | bytes accessed | tf_op | source)
XLA Modules:
  0.0 724.2 jit_solution(13899461857553801861)
XLA Ops:
  7.2 0.0 all-reduce.3.cloned.1.call-start
  7.2 4.3 fusion
  11.5 0.0 all-reduce.3.cloned.1.call-update
  11.5 0.0 all-reduce.5.cloned.1.call-start
  11.6 100.2 %all-reduce.3.cloned.1.call-done = f32[32,2048]{1,0:T(8,128)} async-done(((f32[32,2048]{1,0:T(8,128)}), f32[32,2048]{1,0:T(8,128)}) %all-reduce.3.cloned.1.call-update) | async-done | bytes 262160 | tf_op jit(solution)/shard_map/psum | solution.py:15
  111.8 1.0 multiply_convert_fusion
  112.7 0.0 copy-start
  112.8 0.2 fusion.6
  112.9 3.7 fusion.7
  116.6 209.6 %psum.22 = f32[32,32]{0,1:T(8,128)S(1)} all-reduce(f32[32,32]{0,1:T(8,128)S(1)} %fusion.6), channel_id=1, replica_groups=mesh['space'=64,'tm'=8] {'space'}, use_global_device_ids=true, to_apply=%region_1.0 | all-reduce | flops 1024 | bytes 8192 | tf_op jit(solution)/shard_map/psum | solution.py:21
  326.2 0.1 copy.5
  326.3 2.9 cholesky.16
  329.3 0.6 compare_reduce_fusion
  329.9 0.0 all-reduce.5.cloned.1.call-update
  329.9 0.6 fusion.2
  330.5 2.4 custom-call.7
  332.9 382.6 %all-reduce.5.cloned.1.call-done = f32[32,1024]{1,0:T(8,128)} async-done(((f32[32,1024]{1,0:T(8,128)}), f32[32,1024]{1,0:T(8,128)}) %all-reduce.5.cloned.1.call-update) | async-done | bytes 131088 | tf_op jit(solution)/shard_map/psum | solution.py:22
  715.5 1.9 fusion.3
  717.4 0.0 copy-done
  (2 shorter events, 0.0 us)
Async XLA Ops:
  7.2 104.6 %all-reduce.3.cloned.1.call-start = ((), (), s32[]{:S(2)}) async-start(), calls=%async_computation | async-start | bytes 524288 | tf_op jit(solution)/shard_map/psum | solution.py:15
  11.5 704.0 %all-reduce.5.cloned.1.call-start = ((), (), s32[]{:S(2)}) async-start(), calls=%async_computation.1 | async-start | bytes 262144 | tf_op jit(solution)/shard_map/psum | solution.py:22
  112.7 604.7 %copy-start = (bf16[32,2048]{1,0:T(8,128)(2,1)}, bf16[32,2048]{1,0:T(8,128)(2,1)S(1)}, u32[]{:S(2)}) copy-start(bf16[32,2048]{1,0:T(8,128)(2,1)S(1)} %multiply_convert_fusion) | copy-start | bytes 393220
Sparse Core Ops, SparseCore 0:
  11.7 100.0 all-reduce.2
  330.0 385.4 all-reduce.4
where the time goes:
time: 724 us
  waiting for transfers between devices  483 us (67%)
  blocking collectives  210 us (29%)
  between operations  14.1 us (2%)
  matrix products  10 us (1%)
  other arithmetic  7.57 us (1%)
    psum x1, waiting for transfers between devices, per_device(): projection = lax.psum(proj_part, 'space')  383 us
    psum x1, blocking collectives, per_device(): gram = lax.psum(gram_part, 'space')  210 us
    psum x1, waiting for transfers between devices, per_device(): summed = lax.psum(partial_sums, 'tm')  100 us
  transfers between devices with their start and end apart: 2, of which 2 were waited for; matrix products, arithmetic and copies ran while one was open for 0% of the time, Pallas kernels for 0%

commit v1 on v0

--- a/solution.py
+++ b/solution.py
@@ -18,7 +18,7 @@
         sketch, sketch, (((1,), (1,)), ((), ())), preferred_element_type=jnp.float32
     )
     proj_part = jnp.dot(sketch, snapshots, preferred_element_type=jnp.float32)
-    gram = lax.psum(gram_part, "space")
+    gram = jnp.sum(lax.all_gather(gram_part, "space"), axis=0)
     projection = lax.psum(proj_part, "space")
     lower = jnp.linalg.cholesky(gram)
     coefficients = jax.scipy.linalg.solve_triangular(lower, projection, lower=True)

time: 724 us -> 581 us (0.80)
  blocking collectives: 210 us -> 72.3 us
    psum x1 -> x0, blocking collectives: 210 us -> none  [per_device(): gram = lax.psum(gram_part, 'space')]
    all_gather x0 -> x1, blocking collectives: none -> 72.3 us  [per_device(): gram = jnp.sum(lax.all_gather(gram_part, 'space'), axis=0)]
  transfers between devices with their start and end apart: 2 -> 2, of which waited for: 2 -> 2; matrix products, arithmetic and copies ran while one was open for 0% -> 1% of each run, Pallas kernels for 0% -> 0%
where the time goes in v1:
time: 581 us
  waiting for transfers between devices  477 us (82%)
  blocking collectives  72.3 us (12%)
  between operations  14.1 us (2%)
  matrix products  10 us (2%)
  other arithmetic  7.67 us (1%)
    psum x1, waiting for transfers between devices, per_device(): projection = lax.psum(proj_part, 'space')  377 us
    psum x1, waiting for transfers between devices, per_device(): summed = lax.psum(partial_sums, 'tm')  100 us
    all_gather x1, blocking collectives, per_device(): gram = jnp.sum(lax.all_gather(gram_part, 'space'), axis=0)  72.3 us
  transfers between devices with their start and end apart: 2, of which 2 were waited for; matrix products, arithmetic and copies ran while one was open for 1% of the time, Pallas kernels for 0%

profile of v1, /device:TPU:1, one launch (start us, length us, event | category | flops | bytes accessed | tf_op | source)
XLA Modules:
  0.0 580.9 jit_solution(12229639972923265290)
XLA Ops:
  7.2 0.0 all-reduce.3.cloned.1.call-start
  7.2 4.3 fusion
  11.5 0.0 all-reduce.3.cloned.1.call-update
  11.5 0.0 all-reduce.5.cloned.1.call-start
  11.6 100.2 %all-reduce.3.cloned.1.call-done = f32[32,2048]{1,0:T(8,128)} async-done(((f32[32,2048]{1,0:T(8,128)}), f32[32,2048]{1,0:T(8,128)}) %all-reduce.3.cloned.1.call-update) | async-done | bytes 262160 | tf_op jit(solution)/shard_map/psum | solution.py:15
  111.8 1.0 multiply_convert_fusion
  112.7 0.0 copy-start
  112.8 0.2 fusion.6
  112.9 3.7 fusion.7
  116.6 72.3 %all-gather = f32[2048,32]{1,0:T(8,128)S(1)} all-gather(f32[32,32]{1,0:T(8,128)S(1)} %fusion.6), channel_id=2, replica_groups=mesh['space'=64,'tm'=8] {'space'}, dimensions={0}, use_global_device_ids=true | all-gather | bytes 266240 | tf_op jit(solution)/shard_map/all_gather | solution.py:21
  188.9 0.1 reduce_sum.9
  189.0 0.1 copy.5
  189.1 2.9 cholesky.16
  192.0 0.6 compare_reduce_fusion
  192.6 0.0 all-reduce.5.cloned.1.call-update
  192.7 0.6 fusion.2
  193.2 2.4 custom-call.7
  195.7 376.5 %all-reduce.5.cloned.1.call-done = f32[32,1024]{1,0:T(8,128)} async-done(((f32[32,1024]{1,0:T(8,128)}), f32[32,1024]{1,0:T(8,128)}) %all-reduce.5.cloned.1.call-update) | async-done | bytes 131088 | tf_op jit(solution)/shard_map/psum | solution.py:22
  572.2 1.9 fusion.3
  574.1 0.0 copy-done
  (2 shorter events, 0.0 us)
Async XLA Ops:
  7.2 104.6 %all-reduce.3.cloned.1.call-start = ((), (), s32[]{:S(2)}) async-start(), calls=%async_computation | async-start | bytes 524288 | tf_op jit(solution)/shard_map/psum | solution.py:15
  11.5 560.7 %all-reduce.5.cloned.1.call-start = ((), (), s32[]{:S(2)}) async-start(), calls=%async_computation.1 | async-start | bytes 262144 | tf_op jit(solution)/shard_map/psum | solution.py:22
  112.7 461.3 %copy-start = (bf16[32,2048]{1,0:T(8,128)(2,1)}, bf16[32,2048]{1,0:T(8,128)(2,1)S(1)}, u32[]{:S(2)}) copy-start(bf16[32,2048]{1,0:T(8,128)(2,1)S(1)} %multiply_convert_fusion) | copy-start | bytes 393220
Sparse Core Ops, SparseCore 0:
  11.7 100.0 all-reduce.2
  192.8 379.3 all-reduce.4
